TPU v7x, 512 devices: a whole 4x8x8 slice. The times are simulated.
512 devices in a mesh: seq: 8 (over z), vocab: 64 (over y, x, core).
Axes of the slice: x: 4, y: 8, z: 8, core: 2. Of those that a mesh axis runs over, the one named last changes fastest.
Arguments:
- hidden: bfloat16 [2048, 8192], P('seq', 'vocab'), may hold values from -120 to 120
- head_weight: bfloat16 [8192, 98304], P('seq', 'vocab'), may hold values from -0.0625 to 0.0625
- vocab_basis: bfloat16 [98304, 1024], P('vocab', 'seq'), may hold values from -0.0048828125 to 0.0048828125
- keep_index: int32 [512], P('seq'), may hold values from 0 to 255, as said below
- counts: int32 [8], P('seq'), may hold values from 1 to 64, as said below
Outputs:
- coefficients: float32 [512, 1024], P('seq', 'vocab')
Inputs may be any that keep to these rules, and one draw needn't show every extreme that they name: `keep_index`: each owner's list is strictly increasing and ends at 255. `counts`: exactly one owner has all 64 slots live.
All inputs are finite; a program needn't handle non-finite values.
Results may differ from a plain program's by a relative error of at most 0.0032.
Values may be sent and summed in bfloat16 or wider, within the bound.
No kernel may reach another device: no remote copies, remote signals or barrier semaphores. Data moves between devices by JAX's collectives and lax.ppermute only.
A program may use at most 64 MiB of HBM per device.

v0:
```python
import jax
import jax.numpy as jnp
from jax import lax
from jax.sharding import PartitionSpec as P


def shards(hidden, head_weight, vocab_basis, keep_index, counts):
    chosen = jnp.take(hidden, keep_index, axis=0)
    features = lax.all_gather(chosen, "vocab", axis=1, tiled=True)
    pieces = lax.all_to_all(features, "seq", split_axis=1, concat_axis=0, tiled=True)
    owned = features.shape[0]
    logits = lax.psum_scatter(
        jnp.dot(pieces, head_weight, preferred_element_type=jnp.float32),
        "seq",
        scatter_dimension=0,
        tiled=True,
    )
    row_max = lax.pmax(jnp.max(logits, axis=1, keepdims=True), "vocab")
    weights = jnp.exp(logits - row_max)
    denominator, weighted = lax.psum(
        (jnp.sum(weights, axis=1, keepdims=True), jnp.sum(weights * logits, axis=1, keepdims=True)),
        "vocab",
    )
    expected = weighted / denominator
    centred = (logits - expected).astype(jnp.bfloat16)
    partial_sums = jnp.dot(
        centred,
        lax.all_gather(vocab_basis, "seq", axis=1, tiled=True),
        preferred_element_type=jnp.float32,
    )
    summed = lax.psum_scatter(partial_sums, "vocab", scatter_dimension=1, tiled=True)
    live_rows = jnp.arange(owned, dtype=jnp.int32) < counts[0]
    return jnp.where(live_rows[:, None], summed, jnp.float32(0.0))


def solution(mesh):
    in_specs = (P("seq", "vocab"), P("seq", "vocab"), P("vocab", "seq"), P("seq"), P("seq"))
    out_specs = P("seq", "vocab")
    return jax.shard_map(shards, mesh=mesh, in_specs=in_specs, out_specs=out_specs, check_vma=False)
```

profile of v0, /device:TPU:2, one launch (start us, length us, event | category | flops | bytes accessed | tf_op | source)
XLA Modules:
  0.0 629.6 jit_solution(8558448056872284931)
XLA Ops:
  6.5 0.0 copy-start
  6.5 0.0 all-gather.3.cloned.1.call-start
  6.5 0.8 compare_select_fusion
  7.3 0.8 compare_and_fusion
  8.2 1.5 gather_fusion
  9.6 0.7 broadcast_select_fusion
  10.3 0.0 all-gather.3.cloned.1.call-update
  10.3 0.0 reduce-scatter.2.cloned.1.call-start
  10.4 80.3 %all-gather.3.cloned.1.call-done = bf16[64,8192]{1,0:T(8,128)(2,1)} async-done(((bf16[64,128]{1,0:T(8,128)(2,1)}), bf16[64,8192]{1,0:T(8,128)(2,1)}) %all-gather.3.cloned.1.call-update) | async-done | bytes 1048592 | tf_op jit(solution)/shard_map/all_gather | solution.py:9
  90.7 1.3 copy.10
  92.0 36.3 %all_to_all.19 = bf16[64,8,1024]{2,0,1:T(8,128)(2,1)S(1)} all-to-all(bf16[64,8,1024]{2,0,1:T(8,128)(2,1)S(1)} %bitcast.17), channel_id=1, replica_groups=mesh['seq'=8,'vocab'=64] {'seq'}, dimensions={1} | all-to-all | bytes 2097152 | tf_op jit(solution)/shard_map/all_to_all | solution.py:10
  128.3 0.0 copy-done
  128.3 3.5 fusion.3
  131.8 0.0 reduce-scatter.2.cloned.1.call-update
  131.8 0.0 all-gather.5.cloned.1.call-start
  131.9 0.7 all-gather.5.cloned.1.call-update
  132.6 0.0 all-reduce.4.cloned.1.call-start
  132.6 43.5 %reduce-scatter.2.cloned.1.call-done = f32[64,1536]{1,0:T(8,128)} async-done(((f32[512,1536]{1,0:T(8,128)}), f32[64,1536]{1,0:T(8,128)}) %reduce-scatter.2.cloned.1.call-update) | async-done | bytes 393232 | tf_op jit(solution)/shard_map/reduce_scatter | solution.py:12
  176.1 1.1 reduce_max.9
  177.2 120.6 %pmax.7 = f32[64]{0:T(128)S(1)} all-reduce(f32[64]{0:T(128)S(1)} %reduce_max.9), channel_id=1, replica_groups=mesh['seq'=8,'vocab'=64] {'vocab'}, use_global_device_ids=true, to_apply=%region_2.3 | all-reduce | flops 64 | bytes 512 | tf_op jit(solution)/shard_map/pmax | solution.py:18
  297.8 1.2 fusion
  299.1 124.1 %all-reduce.1 = (f32[64,1]{0,1:T(1,128)S(1)}, f32[64,1]{0,1:T(1,128)S(1)}) all-reduce(f32[64,1]{0,1:T(1,128)S(1)} %bitcast.21, f32[64,1]{0,1:T(1,128)S(1)} %bitcast.20), channel_id=1, replica_groups=mesh['seq'=8,'vocab'=64] {'vocab'}, use_global_device_ids=true, to_apply=%region_4.5 | all-reduce | flops 128 | bytes 1024 | tf_op jit(solution)/shard_map/psum | solution.py:20
  423.1 0.0 all-gather.5.cloned.1.call-done
  423.2 4.2 fusion.1
  427.3 0.0 all-reduce.4.cloned.1.call-update
  428.0 1.3 dynamic-slice
  429.9 191.8 %all-reduce.4.cloned.1.call-done = f32[64,1024]{0,1:T(8,128)} async-done(((f32[64,1024]{0,1:T(8,128)}), f32[64,1024]{0,1:T(8,128)}) %all-reduce.4.cloned.1.call-update) | async-done | bytes 262160
  621.7 1.3 dynamic-slice_select_fusion
  (3 shorter events, 0.0 us)
Async XLA Ops:
  6.5 121.8 %copy-start = (bf16[1024,1536]{1,0:T(8,128)(2,1)S(1)}, bf16[1024,1536]{1,0:T(8,128)(2,1)}, u32[]{:S(2)}) copy-start(bf16[1024,1536]{1,0:T(8,128)(2,1)} %param.6) | copy-start | bytes 9437188
  6.5 84.1 %all-gather.3.cloned.1.call-start = ((), (), s32[]{:S(2)}) async-start(), calls=%async_computation.2 | async-start | bytes 1064960 | tf_op jit(solution)/shard_map/all_gather | solution.py:9
  10.3 165.7 %reduce-scatter.2.cloned.1.call-start = ((), (), s32[]{:S(2)}) async-start(), calls=%async_computation.3 | async-start | bytes 3538944 | tf_op jit(solution)/shard_map/reduce_scatter | solution.py:12
  131.8 291.3 %all-gather.5.cloned.1.call-start = ((), (), s32[]{:S(2)}) async-start(), calls=%async_computation.4 | async-start | bytes 3538944 | tf_op jit(solution)/shard_map/all_gather | solution.py:28
  132.6 489.2 %all-reduce.4.cloned.1.call-start = ((), (), s32[]{:S(2)}) async-start(), calls=%async_computation.5 | async-start | bytes 1048576
Sparse Core Ops, SparseCore 0:
  10.6 80.0 all-gather.2
  131.9 44.0 reduce-scatter.1
  178.1 57.3 all-gather.4
  427.5 194.2 all-reduce.3
where the time goes:
time: 630 us
  waiting for transfers between devices  316 us (50%)
  blocking collectives  281 us (45%)
  between operations  14.5 us (2%)
  matrix products  7.68 us (1%)
    unnamed x5, waiting for transfers between devices  193 us
    psum x1, blocking collectives, shards(): lax.psum((jnp.sum(weights, axis=1, keepdims=True), jnp.sum(weights * logi...  124 us
    pmax x1, blocking collectives, shards(): row_max = lax.pmax(jnp.max(logits, axis=1, keepdims=True), 'vocab')  121 us
    all_gather x1, waiting for transfers between devices, shards(): features = lax.all_gather(chosen, 'vocab', axis=1, tiled=True)  80.3 us
    reduce_scatter x1, waiting for transfers between devices, shards(): lax.psum_scatter(jnp.dot(pieces, head_weight, preferred_element_type=jnp....  43.5 us
    all_to_all x1, blocking collectives, shards(): lax.all_to_all(features, 'seq', split_axis=1, concat_axis=0, tiled=True)  36.3 us
  transfers between devices with their start and end apart: 4, of which 3 were waited for; matrix products, arithmetic and copies ran while one was open for 1% of the time, Pallas kernels for 0%

commit v1 on v0

--- a/solution.py
+++ b/solution.py
@@ -6,7 +6,11 @@
 
 def shards(hidden, head_weight, vocab_basis, keep_index, counts):
     chosen = jnp.take(hidden, keep_index, axis=0)
-    features = lax.all_gather(chosen, "vocab", axis=1, tiled=True)
+    count = lax.axis_size("vocab")
+    repeats = [count if d == 1 else 1 for d in range(chosen.ndim)]
+    features = lax.all_to_all(
+        jnp.tile(chosen, repeats), "vocab", split_axis=1, concat_axis=1, tiled=True
+    )
     pieces = lax.all_to_all(features, "seq", split_axis=1, concat_axis=0, tiled=True)
     owned = features.shape[0]
     logits = lax.psum_scatter(

time: 630 us -> 593 us (0.941)
  waiting for transfers between devices: 316 us -> 235 us
  blocking collectives: 281 us -> 322 us
    all_gather x1 -> x0, waiting for transfers between devices: 80.3 us -> none  [shards(): features = lax.all_gather(chosen, 'vocab', axis=1, tiled=True)]
    all_to_all x0 -> x1, blocking collectives: none -> 39.2 us  [shards(): lax.all_to_all(jnp.tile(chosen, repeats), 'vocab', split_axis=1, concat_a...]
    unnamed x5 -> x4, waiting for transfers between devices: 193 us -> 193 us
  transfers between devices with their start and end apart: 4 -> 3, of which waited for: 3 -> 2; matrix products, arithmetic and copies ran while one was open for 1% -> 1% of each run, Pallas kernels for 0% -> 0%
where the time goes in v1:
time: 593 us; the launch traced here: 592 us
  blocking collectives  322 us (54%)
  waiting for transfers between devices  235 us (40%)
  between operations  14.4 us (2%)
  local copies, waits for them, and re-layouts  8.76 us (1%)
  matrix products  7.68 us (1%)
    unnamed x4, waiting for transfers between devices  193 us
    psum x1, blocking collectives, shards(): lax.psum((jnp.sum(weights, axis=1, keepdims=True), jnp.sum(weights * logi...  124 us
    pmax x1, blocking collectives, shards(): row_max = lax.pmax(jnp.max(logits, axis=1, keepdims=True), 'vocab')  120 us
    reduce_scatter x1, waiting for transfers between devices, shards(): lax.psum_scatter(jnp.dot(pieces, head_weight, preferred_element_type=jnp....  41.7 us
    all_to_all x1, blocking collectives, shards(): lax.all_to_all(jnp.tile(chosen, repeats), 'vocab', split_axis=1, concat_a...  39.2 us
    all_to_all x1, blocking collectives, shards(): lax.all_to_all(features, 'seq', split_axis=1, concat_axis=0, tiled=True)  37.9 us
  transfers between devices with their start and end apart: 3, of which 2 were waited for; matrix products, arithmetic and copies ran while one was open for 1% of the time, Pallas kernels for 0%

profile of v1, /device:TPU:2, one launch (start us, length us, event | category | flops | bytes accessed | tf_op | source)
XLA Modules:
  0.0 592.5 jit_solution(5772289169299730955)
XLA Ops:
  6.5 0.0 copy-start
  6.5 0.0 reduce-scatter.2.cloned.1.call-start
  6.5 0.8 compare_select_fusion
  7.3 0.8 compare_and_fusion
  8.2 1.5 gather_fusion
  9.6 0.1 broadcast_select_fusion
  9.7 0.2 tile.2
  10.0 39.2 %all_to_all.25 = bf16[64,64,128]{2,0,1:T(8,128)(2,1)S(1)} all-to-all(bf16[64,64,128]{2,0,1:T(8,128)(2,1)S(1)} %tile.2), channel_id=1, replica_groups=mesh['seq'=8,'vocab'=64] {'vocab'}, dimensions={1} | all-to-all | bytes 2097152 | tf_op jit(solution)/shard_map/all_to_all | solution.py:11
  49.2 1.7 copy.7
  50.8 2.3 all_to_all.19
  53.1 1.8 copy.8
  55.0 37.9 %all_to_all.26 = bf16[64,8,1024]{2,0,1:T(8,128)(2,1)S(1)} all-to-all(bf16[64,8,1024]{2,0,1:T(8,128)(2,1)S(1)} %copy.8), channel_id=1, replica_groups=mesh['seq'=8,'vocab'=64] {'seq'}, dimensions={1} | all-to-all | bytes 2097152 | tf_op jit(solution)/shard_map/all_to_all | solution.py:14
  92.8 0.0 copy-done
  92.8 3.5 fusion.3
  96.3 0.0 reduce-scatter.2.cloned.1.call-update
  96.4 0.0 all-gather.2.cloned.1.call-start
  96.4 0.7 all-gather.2.cloned.1.call-update
  97.1 0.0 all-reduce.4.cloned.1.call-start
  97.2 41.7 %reduce-scatter.2.cloned.1.call-done = f32[64,1536]{1,0:T(8,128)} async-done(((f32[512,1536]{1,0:T(8,128)}), f32[64,1536]{1,0:T(8,128)}) %reduce-scatter.2.cloned.1.call-update) | async-done | bytes 393232 | tf_op jit(solution)/shard_map/reduce_scatter | solution.py:16
  138.9 1.1 reduce_max.9
  140.0 120.4 %pmax.7 = f32[64]{0:T(128)S(1)} all-reduce(f32[64]{0:T(128)S(1)} %reduce_max.9), channel_id=1, replica_groups=mesh['seq'=8,'vocab'=64] {'vocab'}, use_global_device_ids=true, to_apply=%region_2.3 | all-reduce | flops 64 | bytes 512 | tf_op jit(solution)/shard_map/pmax | solution.py:22
  260.5 1.2 fusion
  261.7 124.1 %all-reduce.1 = (f32[64,1]{0,1:T(1,128)S(1)}, f32[64,1]{0,1:T(1,128)S(1)}) all-reduce(f32[64,1]{0,1:T(1,128)S(1)} %bitcast.15, f32[64,1]{0,1:T(1,128)S(1)} %bitcast.14), channel_id=1, replica_groups=mesh['seq'=8,'vocab'=64] {'vocab'}, use_global_device_ids=true, to_apply=%region_4.5 | all-reduce | flops 128 | bytes 1024 | tf_op jit(solution)/shard_map/psum | solution.py:24
  385.8 0.0 all-gather.2.cloned.1.call-done
  385.8 4.2 fusion.1
  390.0 0.0 all-reduce.4.cloned.1.call-update
  390.6 1.3 dynamic-slice
  392.6 192.1 %all-reduce.4.cloned.1.call-done = f32[64,1024]{0,1:T(8,128)} async-done(((f32[64,1024]{0,1:T(8,128)}), f32[64,1024]{0,1:T(8,128)}) %all-reduce.4.cloned.1.call-update) | async-done | bytes 262160
  584.6 1.3 dynamic-slice_select_fusion
  (3 shorter events, 0.0 us)
Async XLA Ops:
  6.5 86.3 %copy-start = (bf16[1024,1536]{1,0:T(8,128)(2,1)S(1)}, bf16[1024,1536]{1,0:T(8,128)(2,1)}, u32[]{:S(2)}) copy-start(bf16[1024,1536]{1,0:T(8,128)(2,1)} %param.6) | copy-start | bytes 9437188
  6.5 132.4 %reduce-scatter.2.cloned.1.call-start = ((), (), s32[]{:S(2)}) async-start(), calls=%async_computation.3 | async-start | bytes 3538944 | tf_op jit(solution)/shard_map/reduce_scatter | solution.py:16
  96.4 289.4 %all-gather.2.cloned.1.call-start = ((), (), s32[]{:S(2)}) async-start(), calls=%async_computation.4 | async-start | bytes 3538944 | tf_op jit(solution)/shard_map/all_gather | solution.py:32
  97.1 487.5 %all-reduce.4.cloned.1.call-start = ((), (), s32[]{:S(2)}) async-start(), calls=%async_computation.5 | async-start | bytes 1048576
Sparse Core Ops, SparseCore 0:
  96.5 42.3 reduce-scatter.1
  140.9 57.4 all-gather.1
  390.1 194.5 all-reduce.3
